TPU v7x, 256 devices: a whole 4x4x8 slice. The times are simulated.
256 devices in a mesh: dp: 4 (over x), tensor: 64 (over y, z, core).
Axes of the slice: x: 4, y: 4, z: 8, core: 2. Of those that a mesh axis runs over, the one named last changes fastest.
Arguments:
- grad_out: bfloat16 [4096, 8192], P('dp', 'tensor'), may hold values from -6 to 6
- acts: bfloat16 [4096, 16384], P('dp', 'tensor'), may hold values from -6 to 6
- weight: bfloat16 [8192, 16384], P('tensor'), may hold values from -0.078125 to 0.078125
- block_mask: int32 [64, 128], replicated, may hold values from 0 to 1, as said below
Outputs:
- grad_acts: bfloat16 [4096, 16384], P('dp', 'tensor')
- grad_weight: float32 [8192, 16384], P(('dp', 'tensor'))
Inputs may be any that keep to these rules, and one draw needn't show every extreme that they name: `block_mask`: kept shares differ between groups of 2 consecutive block columns, from about three twentieths to nine twentieths.
All inputs are finite; a program needn't handle non-finite values.
Results may differ from a plain program's by a relative error of at most 0.001.
Values may be sent and summed in bfloat16 or wider, within the bound.
A program may use at most 128 MiB of HBM per device.

v0:
```python
import jax
import jax.numpy as jnp
from jax import lax
from jax.sharding import PartitionSpec as P


def expand_mask(mask, side):
    rows, cols = mask.shape
    full = jnp.broadcast_to(mask[:, None, :, None], (rows, side, cols, side))
    return full.reshape(rows * side, cols * side)


def body(grad_out, acts, weight, block_mask):
    tensor_count = lax.axis_size("tensor")
    group_count = lax.axis_size("dp")
    position = lax.axis_index("tensor")
    d_tile = weight.shape[0]
    full_width = weight.shape[1]
    ff_tile = acts.shape[1]
    side = full_width // block_mask.shape[1]
    total_rows = d_tile * tensor_count
    row_mask = lax.dynamic_slice_in_dim(block_mask, position * (d_tile // side), d_tile // side, 0)
    kept = weight * expand_mask(row_mask, side).astype(jnp.bfloat16)
    columns = lax.all_to_all(kept, "tensor", split_axis=1, concat_axis=0, tiled=True)
    piece = lax.all_gather(grad_out, "tensor", axis=1, tiled=True)
    input_grad = jnp.dot(piece, columns, preferred_element_type=jnp.float32)
    grad_rows = lax.dot_general(
        piece, acts, (((0,), (0,)), ((), ())), preferred_element_type=jnp.float32
    )
    weight_grad = grad_rows
    input_grad, weight_grad = (input_grad, weight_grad)
    grad_acts = input_grad.astype(jnp.bfloat16)
    col_mask = lax.dynamic_slice_in_dim(
        block_mask, position * (ff_tile // side), ff_tile // side, 1
    )
    scale_factor = 1.0 / (grad_out.shape[0] * group_count) ** 0.5
    weight_grad = weight_grad * expand_mask(col_mask, side).astype(jnp.float32) * scale_factor
    quarter = total_rows // (group_count * tensor_count)
    reordered = weight_grad.reshape(group_count, tensor_count, quarter, ff_tile)
    reordered = jnp.transpose(reordered, (1, 0, 2, 3)).reshape(total_rows, ff_tile)
    owned = lax.all_to_all(reordered, "tensor", split_axis=0, concat_axis=1, tiled=True)
    grad_weight = lax.psum_scatter(owned, "dp", scatter_dimension=0, tiled=True)
    return (grad_acts, grad_weight)


def solution(mesh):
    in_specs = (P("dp", "tensor"), P("dp", "tensor"), P("tensor", None), P())
    out_specs = (P("dp", "tensor"), P(("dp", "tensor"), None))
    return jax.shard_map(body, mesh=mesh, in_specs=in_specs, out_specs=out_specs, check_vma=False)
```

profile of v0, /device:TPU:8, one launch (start us, length us, event | category | flops | bytes accessed | tf_op | source)
XLA Modules:
  0.0 494.8 jit_solution(10132291511642374837)
XLA Ops:
  7.2 0.0 copy-start
  7.2 0.0 all-gather.2.cloned.1.call-start
  7.2 0.7 all-gather.2.cloned.1.call-update
  7.9 0.0 reduce-scatter.4.cloned.1.call-start
  8.0 0.8 dynamic-slice_convert_fusion
  8.8 110.2 %all-gather.2.cloned.1.call-done = bf16[1024,8192]{1,0:T(8,128)(2,1)} async-done(((bf16[1024,128]{1,0:T(8,128)(2,1)}), bf16[1024,8192]{1,0:T(8,128)(2,1)}) %all-gather.2.cloned.1.call-update) | async-done | bytes 16777232 | tf_op jit(solution)/shard_map/all_gather | solution.py:25
  119.0 5.5 %broadcast_in_dim.16 = f32[64,128,2,128]{3,2,1,0:T(2,128)} broadcast(f32[64,2]{1,0:T(8,128)S(1)} %dynamic-slice_convert_fusion), dimensions={0,2} | broadcast | bytes 8389120 | tf_op jit(solution)/shard_map/broadcast_in_dim | solution.py:9
  124.5 0.0 copy-done
  124.5 13.7 %fusion = f32[8192,256]{1,0:T(8,128)S(1)} fusion(bf16[1024,8192]{1,0:T(8,128)(2,1)} %all-gather.2.cloned.1.call-done, bf16[1024,256]{1,0:T(8,128)(2,1)S(1)} %copy-done, f32[1024,8,2,128]{3,2,1,0:T(2,128)} %bitcast.29), kind=kOutput, calls=%fused_computation.1 | convolution fusion | flops 4299161600 | bytes 34078720 | tf_op jit(solution)/shard_map/dot_general | solution.py:27
  138.2 1.7 copy.17
  139.8 192.3 %all_to_all.38 = f32[64,128,256]{2,1,0:T(8,128)} all-to-all(f32[64,128,256]{2,1,0:T(8,128)S(1)} %bitcast.24), channel_id=1, replica_groups=mesh['dp'=4,'tensor'=64] {'tensor'}, dimensions={0} | all-to-all | bytes 16777216 | tf_op jit(solution)/shard_map/all_to_all | solution.py:41
  332.1 9.0 %copy.18 = f32[128,64,256]{0,2,1:T(8,128)} copy(f32[128,64,256]{2,0,1:T(8,128)} %bitcast.25) | data formatting | bytes 16777216 | tf_op jit(solution)/shard_map/all_to_all | solution.py:41
  341.1 9.0 %copy.21 = f32[128,16384]{1,0:T(8,128)} copy(f32[128,16384]{0,1:T(8,128)} %bitcast.26) | data formatting | bytes 16777216
  350.1 0.0 reduce-scatter.4.cloned.1.call-update
  350.1 6.4 %copy.15 = bf16[128,16384]{0,1:T(8,128)(2,1)} copy(bf16[128,16384]{1,0:T(8,128)(2,1)} %param.6) | data formatting | bytes 8388608 | tf_op args[2]
  356.5 0.7 convert_bitcast_fusion
  357.2 0.1 broadcast_bitcast_fusion
  357.3 9.8 %broadcast_multiply_fusion = bf16[128,16384]{0,1:T(8,128)(2,1)S(1)} fusion(bf16[128,16384]{0,1:T(8,128)(2,1)} %copy.15, bf16[16384]{0:T(1024)(128)(2,1)S(1)} %broadcast_bitcast_fusion), kind=kLoop, calls=%fused_computation.2 | loop fusion | flops 2097152 | bytes 8421376 | tf_op jit(solution)/shard_map/mul | solution.py:23
  367.1 101.9 %all_to_all.39 = bf16[128,64,256]{0,2,1:T(8,128)(2,1)} all-to-all(bf16[128,64,256]{0,2,1:T(8,128)(2,1)S(1)} %bitcast.27), channel_id=1, replica_groups=mesh['dp'=4,'tensor'=64] {'tensor'}, dimensions={1} | all-to-all | bytes 8388608 | tf_op jit(solution)/shard_map/all_to_all | solution.py:24
  469.0 6.4 %copy.16 = bf16[64,128,256]{2,1,0:T(8,128)(2,1)} copy(bf16[64,128,256]{1,2,0:T(8,128)(2,1)} %bitcast.28) | data formatting | bytes 8388608 | tf_op jit(solution)/shard_map/all_to_all | solution.py:24
  475.3 0.0 copy-start.1
  475.3 11.6 %fusion.1 = bf16[1024,256]{0,1:T(8,128)(2,1)S(1)} fusion(bf16[8192,256]{1,0:T(8,128)(2,1)} %bitcast.31, bf16[1024,8192]{1,0:T(8,128)(2,1)} %all-gather.2.cloned.1.call-done), kind=kOutput, calls=%fused_computation.4 | convolution fusion | flops 4295229440 | bytes 21495808 | tf_op jit(solution)/shard_map/dot_general | solution.py:26
  487.0 1.0 copy.19
  488.0 0.0 copy-done.1
  (1 shorter events, 0.0 us)
Async XLA Ops:
  7.2 117.3 %copy-start = (bf16[1024,256]{1,0:T(8,128)(2,1)S(1)}, bf16[1024,256]{1,0:T(8,128)(2,1)}, u32[]{:S(2)}) copy-start(bf16[1024,256]{1,0:T(8,128)(2,1)} %param.5) | copy-start | bytes 1572868
  7.2 111.9 %all-gather.2.cloned.1.call-start = ((), (), s32[]{:S(2)}) async-start(), calls=%async_computation.3 | async-start | bytes 17039360 | tf_op jit(solution)/shard_map/all_gather | solution.py:25
  7.9 480.1 %reduce-scatter.4.cloned.1.call-start = ((), (), s32[]{:S(2)}) async-start(), calls=%async_computation.4 | async-start | bytes 10485760
  475.3 12.7 %copy-start.1 = (bf16[1024,256]{1,0:T(8,128)(2,1)S(1)}, bf16[1024,256]{1,0:T(8,128)(2,1)}, u32[]{:S(2)}) copy-start(bf16[1024,256]{1,0:T(8,128)(2,1)} %param.5) | copy-start | bytes 1572868
Sparse Core Ops, SparseCore 0:
  10.6 108.4 all-gather.1
  350.2 81.2 reduce-scatter.3
where the time goes:
time: 498 us; the launch traced here: 495 us
  blocking collectives  294 us (59%)
  waiting for transfers between devices  111 us (22%)
  local copies, waits for them, and re-layouts  38.9 us (8%)
  matrix products  25.3 us (5%)
  between operations  14.1 us (3%)
  other arithmetic  11.4 us (2%)
    all_to_all x1, blocking collectives, body(): lax.all_to_all(reordered, 'tensor', split_axis=0, concat_axis=1, tiled=True)  192 us
    all_gather x1, waiting for transfers between devices, body(): piece = lax.all_gather(grad_out, 'tensor', axis=1, tiled=True)  110 us
    all_to_all x1, blocking collectives, body(): lax.all_to_all(kept, 'tensor', split_axis=1, concat_axis=0, tiled=True)  102 us
    unnamed x7, local copies, waits for them, and re-layouts  16.3 us
    dot_general x1, matrix products, body(): lax.dot_general(piece, acts, (((0,), (0,)), ((), ())), preferred_element_...  13.7 us
    dot_general x1, matrix products, body(): input_grad = jnp.dot(piece, columns, preferred_element_type=jnp.float32)  11.6 us
  transfers between devices with their start and end apart: 2, of which 1 were waited for; matrix products, arithmetic and copies ran while one was open for 7% of the time, Pallas kernels for 0%

commit v1 on v0

v1 whole, which is shorter than its diff:
```python
import jax
import jax.numpy as jnp
from jax import lax
from jax.experimental import pallas as pl
from jax.experimental.pallas import tpu as pltpu
from jax.sharding import PartitionSpec as P

NX, NY, NZ = 4, 4, 8
BLK = 128
BF, F32 = jnp.bfloat16, jnp.float32
MESH = pl.DeviceIdType.MESH


def kernel(go, acts, weight, mask, ga, gw, G, A, At, K, part, R, S,
           t_send, a_send, w_send, z_send, y_send, b_send, s_send, r_send,
           t_recv, a_recv, w_recv, z_recv, yp_recv, ym_recv, y2_recv, b_recv, s_recv, r_recv):
    x = lax.axis_index("dp")
    t = lax.axis_index("tensor")
    y, z, c = t // (2 * NZ), (t % (2 * NZ)) // 2, t % 2
    mine = pl.ds(pl.multiple_of(c * BLK, BLK), BLK)
    other = pl.ds(pl.multiple_of((1 - c) * BLK, BLK), BLK)
    columns = pl.ds(pl.multiple_of(t * 2 * BLK, 2 * BLK), 2 * BLK)
    tokens = go.shape[0]
    half = tokens // 2
    mate = y * 2 * NZ + z * 2 + (1 - c)
    up = ((y + 1) % NY) * 2 * NZ + z * 2 + c
    down = ((y + NY - 1) % NY) * 2 * NZ + z * 2 + c
    right = y * 2 * NZ + ((z + 1) % NZ) * 2 + c
    left = y * 2 * NZ + ((z + NZ - 1) % NZ) * 2 + c

    def send(src, dst, send_sem, recv_sem, to_x, to_t):
        pltpu.make_async_remote_copy(
            src_ref=src, dst_ref=dst, send_sem=send_sem, recv_sem=recv_sem,
            device_id=(to_x, to_t), device_id_type=MESH,
        ).start()

    def wait(region, sem):
        pltpu.make_async_copy(region, region, sem).wait()

    home = G.at[x, z, :, mine]

    @pl.when(x != y)
    def _():
        send(go, home, t_send, t_recv, y, x * 2 * NZ + z * 2 + c)

    @pl.when(x == y)
    def _():
        pltpu.make_async_copy(go, home, t_recv).start()

    pltpu.make_async_copy(acts, A.at[x], a_recv).start()
    for step in (1, 3, 2):
        send(acts, A.at[x], a_send, a_recv, (x + step) % NX, t)

    @pl.loop(0, 2 * NZ)
    def _(n):
        to_t = x * 2 * NZ + n
        src = weight.at[:, pl.ds(pl.multiple_of(to_t * 2 * BLK, 2 * BLK), 2 * BLK)]
        dst = K.at[2 * z + c]
        same = (x == y) & (n == 2 * z + c)

        @pl.when(same)
        def _():
            pltpu.make_async_copy(src, dst, w_recv).start()

        @pl.when(jnp.logical_not(same))
        def _():
            send(src, dst, w_send, w_recv, y, to_t)

    def chunk(k):
        return (z + NZ + ((k + 1) // 2) * (1 - 2 * (k % 2))) % NZ

    def stage_z(k):
        zc = chunk(k)
        block = G.at[y, zc, :, mine]

        @pl.when(k == 0)
        def _():
            wait(block, t_recv)

        @pl.when(k > 0)
        def _():
            wait(block, z_recv.at[k])

        @pl.when((k == 0) | ((k % 2 == 1) & (k < 7)))
        def _():
            send(block, block, z_send, z_recv.at[jnp.where(k == 0, 1, k + 2)], x, right)

        @pl.when((k % 2 == 0) & (k < 6))
        def _():
            send(block, block, z_send, z_recv.at[k + 2], x, left)

        send(block, block, y_send, yp_recv.at[k], x, up)
        send(block, block, y_send, ym_recv.at[k], x, down)
        send(block, block, b_send, b_recv.at[k], x, mate)

    def stage_y(k):
        zc = chunk(k)
        below, above = (y + NY - 1) % NY, (y + 1) % NY
        block = G.at[below, zc, :, mine]
        wait(block, yp_recv.at[k])
        piece = G.at[below, zc, pl.ds(0, half), mine]
        send(piece, piece, y_send, y2_recv.at[k], x, up)
        send(block, block, b_send, b_recv.at[k], x, mate)
        block = G.at[above, zc, :, mine]
        wait(block, ym_recv.at[k])
        piece = G.at[above, zc, pl.ds(half, half), mine]
        send(piece, piece, y_send, y2_recv.at[k], x, down)
        send(block, block, b_send, b_recv.at[k], x, mate)

    def stage_far(k):
        block = G.at[(y + 2) % NY, chunk(k), :, mine]
        wait(block, y2_recv.at[k])
        send(block, block, b_send, b_recv.at[k], x, mate)

    def scalar(row, h):
        return mask[x * 2 * NZ + row, 2 * t + h].astype(F32)

    scale_factor = 1.0 / (tokens * NX) ** 0.5

    def stage_weight_grad(k):
        zc = chunk(k)
        wait(G.at[:, zc, :, other], b_recv.at[k])
        total = jnp.dot(At[0], G[0, zc], preferred_element_type=F32)
        for d in range(1, NX):
            total += jnp.dot(At[d], G[d, zc], preferred_element_type=F32)
        total = total.T * scale_factor
        for r in range(2):
            for h in range(2):
                tile = total[r * BLK:(r + 1) * BLK, h * BLK:(h + 1) * BLK] * scalar(2 * zc + r, h)
                S[pl.ds(8 * zc + 4 * r, 4), :, h * BLK:(h + 1) * BLK] = tile.reshape(4, BLK // 4, BLK)

        @pl.loop(0, 8)
        def _(j):
            n = 8 * zc + j

            @pl.when(n == t)
            def _():
                pltpu.make_async_copy(S.at[n], gw.at[:, columns], s_recv).start()

            @pl.when(n != t)
            def _():
                send(S.at[n], gw.at[:, columns], s_send, s_recv, x, n)

    @pl.loop(0, NZ + 4)
    def _(i):
        @pl.when(i < NZ)
        def _():
            stage_z(i)

        @pl.when((i >= 2) & (i < NZ + 2))
        def _():
            stage_y(i - 2)

        @pl.when((i >= 3) & (i < NZ + 3))
        def _():
            stage_far(i - 3)

        @pl.when(i == 4)
        def _():
            wait(A, a_recv)
            for d in range(NX):
                At[d] = A[d].T

        @pl.when(i >= 4)
        def _():
            stage_weight_grad(i - 4)

    wait(K, w_recv)

    @pl.loop(0, 2 * NZ)
    def _(f):
        for h in range(2):
            cols = slice(h * BLK, (h + 1) * BLK)
            K[f, :, cols] = (K[f, :, cols].astype(F32) * scalar(f, h)).astype(BF)

    @pl.loop(0, NX)
    def _(rel):
        d = (y + rel) % NX

        @pl.loop(0, 4)
        def _(r):
            rows = pl.ds(pl.multiple_of(r * (tokens // 4), tokens // 4), tokens // 4)
            total = jnp.dot(G[d, 0, rows], K[0:2].reshape(2 * BLK, 2 * BLK), preferred_element_type=F32)
            for f in range(1, NZ):
                total += jnp.dot(G[d, f, rows], K[2 * f:2 * f + 2].reshape(2 * BLK, 2 * BLK),
                                 preferred_element_type=F32)
            part[d, rows] = total

        @pl.when(d != x)
        def _():
            send(part.at[d], R.at[(x + NX - d) % NX - 1], r_send, r_recv, d, t)

    wait(R, r_recv)

    @pl.loop(0, 8)
    def _(r):
        rows = pl.ds(pl.multiple_of(r * (tokens // 8), tokens // 8), tokens // 8)
        ga[rows] = ((part[x, rows] + R[0, rows]) + (R[1, rows] + R[2, rows])).astype(BF)

    wait(gw, s_recv)

    @pl.when(x != y)
    def _():
        wait(go, t_send)
        wait(K, w_send)

    @pl.when(x == y)
    def _():
        wait(K.at[pl.ds(0, 2 * NZ - 1)], w_send)

    wait(A.at[pl.ds(0, 3)], a_send)
    wait(G.at[0, pl.ds(0, 7), :, pl.ds(0, BLK)], z_send)
    wait(G.at[pl.ds(0, 3), pl.ds(0, 4)], y_send)
    wait(G.at[pl.ds(0, 2)], b_send)
    wait(S.at[pl.ds(0, 63)], s_send)
    wait(R, r_send)


def body(grad_out, acts, weight, block_mask):
    tokens, d_tile = grad_out.shape
    ff_tile = acts.shape[1]
    full_width = weight.shape[1]
    dma = pltpu.SemaphoreType.DMA
    return pl.pallas_call(
        kernel,
        out_shape=(
            jax.ShapeDtypeStruct((tokens, ff_tile), BF),
            jax.ShapeDtypeStruct((d_tile // NX, full_width), F32),
        ),
        in_specs=[pl.BlockSpec(memory_space=pl.ANY)] * 3 + [pl.BlockSpec(memory_space=pltpu.SMEM)],
        out_specs=(pl.BlockSpec(memory_space=pltpu.VMEM), pl.BlockSpec(memory_space=pl.ANY)),
        scratch_shapes=[
            pltpu.VMEM((NX, NZ, tokens, 2 * BLK), BF),
            pltpu.VMEM((NX, tokens, ff_tile), BF),
            pltpu.VMEM((NX, ff_tile, tokens), BF),
            pltpu.VMEM((2 * NZ, BLK, ff_tile), BF),
            pltpu.VMEM((NX, tokens, ff_tile), F32),
            pltpu.VMEM((NX - 1, tokens, ff_tile), F32),
            pltpu.VMEM((8 * NZ, BLK // NX, ff_tile), F32),
        ] + [dma] * 8 + [dma] * 3 + [dma((NZ,))] * 5 + [dma] * 2,
        compiler_params=pltpu.CompilerParams(
            has_side_effects=True, vmem_limit_bytes=52 * 1024 * 1024
        ),
    )(grad_out, acts, weight, block_mask)


def solution(mesh):
    in_specs = (P("dp", "tensor"), P("dp", "tensor"), P("tensor", None), P())
    out_specs = (P("dp", "tensor"), P(("dp", "tensor"), None))
    return jax.shard_map(body, mesh=mesh, in_specs=in_specs, out_specs=out_specs, check_vma=False)
```

time: 498 us -> 235 us (0.47)
  the two profiles are of different devices: /device:TPU:8 before, /device:TPU:231 now
where the time goes in v1:
time: 235 us
  Pallas kernels  227 us (97%)
  local copies, waits for them, and re-layouts  6.58 us (3%)
    pallas_call x1, Pallas kernels, body(): pl.pallas_call(kernel, out_shape=(jax.ShapeDtypeStruct((tokens, ff_tile),...  227 us
    unnamed x8, local copies, waits for them, and re-layouts  6.58 us

profile of v1, /device:TPU:231, one launch (start us, length us, event | category | flops | bytes accessed | tf_op | source)
XLA Modules:
  0.0 234.6 jit_solution(13408805140195328088)
XLA Ops:
  0.6 0.0 copy-start
  0.6 1.0 copy-done
  1.7 0.0 copy-start.1
  1.7 0.9 copy-done.1
  2.6 0.0 copy-start.2
  2.6 0.8 copy-done.2
  3.4 227.4 %shard_map.59 = (bf16[1024,256]{1,0:T(8,128)(2,1)S(1)}, f32[32,16384]{1,0:T(8,128)}) custom-call(bf16[1024,128]{1,0:T(8,128)(2,1)S(1)} %copy-done.1, bf16[1024,256]{1,0:T(8,128)(2,1)S(1)} %copy-done, bf16[128,16384]{1,0:T(8,128)(2,1)} %weight.1, s32[64,128]{1,0:T(8,128)S(1)} %copy-done.2), custom_call_target="tpu_custom_call" | custom-call | tf_op jit(solution)/shard_map/pallas_call | solution.py:224
  230.8 0.8 copy.8
  231.6 3.0 %copy.9 = f32[32,16384]{1,0:T(8,128)} copy(f32[32,16384]{1,0:T(8,128)} %get-tuple-element.5) | data formatting | bytes 4194304
Async XLA Ops:
  0.6 1.0 copy-start
  1.7 0.9 copy-start.1
  2.6 0.8 copy-start.2

commit v2 on v1

v2 whole, which is shorter than its diff:
```python
import jax
import jax.numpy as jnp
from jax import lax
from jax.experimental import pallas as pl
from jax.experimental.pallas import tpu as pltpu
from jax.sharding import PartitionSpec as P

NX, NY, NZ = 4, 4, 8
VSTART, VPASS = 1, 5
LEAD, SLICES = 7, 4
BLK = 128
BF, F32 = jnp.bfloat16, jnp.float32
MESH = pl.DeviceIdType.MESH


def kernel(go, acts, weight, mask, ga, gw, G, A, At, V, K, part, H, R, S,
           t_send, a_send, v_send, w_send, z_send, y_send, b_send, s_send, r_send,
           t_recv, a_recv, v_recv, w_recv, z_recv, yp_recv, ym_recv, y2_recv,
           yq_recv, yn_recv, y3_recv, b_recv, b2_recv, s_recv, h_recv, r_recv):
    x = lax.axis_index("dp")
    t = lax.axis_index("tensor")
    y, z, c = t // (2 * NZ), (t % (2 * NZ)) // 2, t % 2
    mine = pl.ds(pl.multiple_of(c * BLK, BLK), BLK)
    other = pl.ds(pl.multiple_of((1 - c) * BLK, BLK), BLK)
    columns = pl.ds(pl.multiple_of(t * 2 * BLK, 2 * BLK), 2 * BLK)
    tokens = go.shape[0]
    half = tokens // 2
    low, high = pl.ds(0, half), pl.ds(half, half)
    mate = y * 2 * NZ + z * 2 + (1 - c)
    up = ((y + 1) % NY) * 2 * NZ + z * 2 + c
    down = ((y + NY - 1) % NY) * 2 * NZ + z * 2 + c
    right = y * 2 * NZ + ((z + 1) % NZ) * 2 + c
    left = y * 2 * NZ + ((z + NZ - 1) % NZ) * 2 + c

    def send(src, dst, send_sem, recv_sem, to_x, to_t):
        pltpu.make_async_remote_copy(
            src_ref=src, dst_ref=dst, send_sem=send_sem, recv_sem=recv_sem,
            device_id=(to_x, to_t), device_id_type=MESH,
        ).start()

    def wait(region, sem):
        pltpu.make_async_copy(region, region, sem).wait()

    def scalar(row, h):
        return mask[x * 2 * NZ + row, 2 * t + h].astype(F32)

    barrier = pltpu.get_barrier_semaphore()
    partner = x * 2 * NZ + z * 2 + c

    @pl.loop(0, NY * 2 * NZ)
    def _(n):
        @pl.when(n != t)
        def _():
            pl.semaphore_signal(barrier, inc=1, device_id=(x, n), device_id_type=MESH)

    @pl.loop(1, NX)
    def _(step):
        @pl.loop(0, 2 * NZ)
        def _(n):
            pl.semaphore_signal(barrier, inc=1, device_id=((x + step) % NX, y * 2 * NZ + n), device_id_type=MESH)

    @pl.when(x != y)
    def _():
        pl.semaphore_signal(barrier, inc=1, device_id=(y, partner), device_id_type=MESH)

    greeted = NY * 2 * NZ - 1 + (NX - 1) * 2 * NZ

    @pl.when(x != y)
    def _():
        pl.semaphore_wait(barrier, greeted + 1)

    @pl.when(x == y)
    def _():
        pl.semaphore_wait(barrier, greeted)

    home = G.at[x, 0, :, mine]

    @pl.when(x != y)
    def _():
        send(go, home, t_send, t_recv, y, x * 2 * NZ + z * 2 + c)

    @pl.when(x == y)
    def _():
        pltpu.make_async_copy(go, home, t_recv).start()

    east, west = (x + 1) % NX, (x + NX - 1) % NX
    pltpu.make_async_copy(acts, A.at[x], a_recv.at[0]).start()

    def start_acts():
        send(acts, A.at[x], a_send, a_recv.at[1], east, t)
        send(acts, A.at[x], a_send, a_recv.at[2], west, t)

    def pass_acts():
        wait(A.at[west], a_recv.at[1])
        piece = A.at[west, pl.ds(0, half)]
        send(piece, piece, a_send, a_recv.at[3], east, t)
        wait(A.at[east], a_recv.at[2])
        piece = A.at[east, pl.ds(half, half)]
        send(piece, piece, a_send, a_recv.at[3], west, t)

    def finish_acts():
        wait(A.at[x], a_recv.at[0])
        wait(A.at[(x + 2) % NX], a_recv.at[3])
        for d in range(NX):
            At[d] = A[d].T

    quarter = BLK // NX
    wide = V.shape[2]
    strip = weight.at[pl.ds(pl.multiple_of(x * quarter, quarter), quarter)]

    def start_weights():
        for step in range(NY):
            there = (y + step) % NY
            src = strip.at[:, pl.ds(pl.multiple_of(there * wide, wide), wide)]
            if step == 0:
                pltpu.make_async_copy(src, V.at[y], v_recv).start()
            else:
                send(src, V.at[y], v_send, v_recv, x, there * 2 * NZ + 2 * z + c)

    def pass_weights():
        wait(V, v_recv)
        dst = K.at[pl.ds(pl.multiple_of(BLK * (2 * z + c) + quarter * x, quarter), quarter)]

        @pl.loop(0, NX * 2 * NZ)
        def _(m):
            e, n = m // (2 * NZ), m % (2 * NZ)
            src = V.at[e, :, pl.ds(pl.multiple_of(n * 2 * BLK, 2 * BLK), 2 * BLK)]
            same = (e == x) & (n == 2 * z + c)

            @pl.when(same)
            def _():
                pltpu.make_async_copy(src, dst, w_recv).start()

            @pl.when(jnp.logical_not(same))
            def _():
                send(src, dst, w_send, w_recv, e, y * 2 * NZ + n)

    def finish_weights():
        wait(K, w_recv)

        @pl.loop(0, 2 * NZ)
        def _(f):
            rows = pl.ds(pl.multiple_of(f * BLK, BLK), BLK)
            for h in range(2):
                cols = slice(h * BLK, (h + 1) * BLK)
                K[rows, cols] = (K[rows, cols].astype(F32) * scalar(f, h)).astype(BF)

    def chunk(k):
        return (z + NZ + ((k + 1) // 2) * (1 - 2 * (k % 2))) % NZ

    def stage_z(k):
        block = G.at[y, k, :, mine]

        @pl.when(k == 0)
        def _():
            wait(block, t_recv)

        @pl.when(k > 0)
        def _():
            wait(block, z_recv.at[k])

        @pl.when((k == 0) | ((k % 2 == 1) & (k < 7)))
        def _():
            to_k = jnp.where(k == 0, 1, k + 2)
            send(block, G.at[y, to_k, :, mine], z_send, z_recv.at[to_k], x, right)

        @pl.when((k % 2 == 0) & (k < 6))
        def _():
            send(block, G.at[y, k + 2, :, mine], z_send, z_recv.at[k + 2], x, left)

        @pl.when(k < LEAD)
        def _():
            send(block, block, y_send, yp_recv.at[k], x, up)
            send(block, block, y_send, ym_recv.at[k], x, down)

        send(block, block, b_send, b_recv.at[0, k], x, mate)

    below, above, beyond = (y + NY - 1) % NY, (y + 1) % NY, (y + 2) % NY

    def stage_y(k):
        block = G.at[below, k, :, mine]
        wait(block, yp_recv.at[k])
        piece = G.at[below, k, low, mine]
        send(piece, piece, y_send, y2_recv.at[k], x, up)
        send(block, block, b_send, b_recv.at[1, k], x, mate)
        block = G.at[above, k, :, mine]
        wait(block, ym_recv.at[k])
        piece = G.at[above, k, high, mine]
        send(piece, piece, y_send, y2_recv.at[k], x, down)
        send(block, block, b_send, b_recv.at[2, k], x, mate)

    def stage_far(k):
        block = G.at[beyond, k, :, mine]
        wait(block, y2_recv.at[k])
        send(block, block, b_send, b_recv.at[3, k], x, mate)

    late = pl.ds(LEAD, NZ - LEAD)
    size = tokens // SLICES

    def rows_of(j, part_of=None):
        if part_of is None:
            return pl.ds(pl.multiple_of(j * size, size), size)
        return pl.ds(pl.multiple_of(j * size + part_of * (size // 2), size // 2), size // 2)

    def slice_start(j):
        block = G.at[y, late, rows_of(j), mine]
        send(block, block, y_send, yq_recv.at[j], x, up)
        send(block, block, y_send, yn_recv.at[j], x, down)

    def slice_y(j):
        block = G.at[below, late, rows_of(j), mine]
        wait(block, yq_recv.at[j])
        piece = G.at[below, late, rows_of(j, 0), mine]
        send(piece, piece, y_send, y3_recv.at[j], x, up)
        send(block, block, b_send, b2_recv.at[0, j], x, mate)
        block = G.at[above, late, rows_of(j), mine]
        wait(block, yn_recv.at[j])
        piece = G.at[above, late, rows_of(j, 1), mine]
        send(piece, piece, y_send, y3_recv.at[j], x, down)
        send(block, block, b_send, b2_recv.at[1, j], x, mate)

    def slice_far(j):
        block = G.at[beyond, late, rows_of(j), mine]
        wait(block, y3_recv.at[j])
        send(block, block, b_send, b2_recv.at[2, j], x, mate)

    def slice_input_grad(j):
        for kind, d in enumerate((below, above, beyond)):
            wait(G.at[d, late, rows_of(j), other], b2_recv.at[kind, j])

        @pl.loop(0, NX)
        def _(rel):
            d = (x + 2 + rel) % NX
            rows = rows_of(j)
            total = jnp.zeros((size, 2 * BLK), F32)
            for k in range(NZ):
                kept = K[pl.ds(pl.multiple_of(2 * BLK * chunk(k), 2 * BLK), 2 * BLK)]
                total += jnp.dot(G[d, k, rows], kept, preferred_element_type=F32)
            part[d, rows] = total

            @pl.when(rel == 0)
            def _():
                send(part.at[d, rows_of(j, 0)], H.at[0, j], r_send, h_recv.at[0, j], east, t)
                send(part.at[d, rows_of(j, 1)], H.at[1, j], r_send, h_recv.at[1, j], west, t)

            @pl.when(rel == 1)
            def _():
                send(part.at[d, rows_of(j, 0)], R.at[1, rows_of(j, 0)], r_send, r_recv.at[j], west, t)

            @pl.when(rel == 3)
            def _():
                send(part.at[d, rows_of(j, 1)], R.at[0, rows_of(j, 1)], r_send, r_recv.at[j], east, t)

    def slice_pass(j):
        wait(H.at[0, j], h_recv.at[0, j])
        part[east, rows_of(j, 0)] += H[0, j]
        send(part.at[east, rows_of(j, 0)], R.at[0, rows_of(j, 0)], r_send, r_recv.at[j], east, t)
        wait(H.at[1, j], h_recv.at[1, j])
        part[west, rows_of(j, 1)] += H[1, j]
        send(part.at[west, rows_of(j, 1)], R.at[1, rows_of(j, 1)], r_send, r_recv.at[j], west, t)

    def slice_finish(j):
        wait(R.at[:, rows_of(j)], r_recv.at[j])
        rows = rows_of(j)
        ga[rows] = (part[x, rows] + R[0, rows] + R[1, rows]).astype(BF)

    scale_factor = 1.0 / (tokens * NX) ** 0.5

    def stage_weight_grad(k):
        zc = chunk(k)

        @pl.when(k < LEAD)
        def _():
            for kind, d in enumerate((y, below, above, beyond)):
                wait(G.at[d, k, :, other], b_recv.at[kind, k])

        total = jnp.dot(At[0], G[0, k], preferred_element_type=F32)
        for d in range(1, NX):
            total += jnp.dot(At[d], G[d, k], preferred_element_type=F32)
        total = total.T * scale_factor
        for r in range(2):
            for h in range(2):
                tile = total[r * BLK:(r + 1) * BLK, h * BLK:(h + 1) * BLK] * scalar(2 * zc + r, h)
                S[pl.ds(8 * zc + 4 * r, 4), :, h * BLK:(h + 1) * BLK] = tile.reshape(4, BLK // 4, BLK)

        @pl.loop(0, 8)
        def _(j):
            n = 8 * zc + j

            @pl.when(n == t)
            def _():
                pltpu.make_async_copy(S.at[n], gw.at[:, columns], s_recv).start()

            @pl.when(n != t)
            def _():
                send(S.at[n], gw.at[:, columns], s_send, s_recv, x, n)

    @pl.loop(0, LEAD + 4)
    def _(i):
        @pl.when(i < NZ)
        def _():
            stage_z(i)

        @pl.when((i >= 2) & (i < LEAD + 2))
        def _():
            stage_y(i - 2)

        @pl.when(i == LEAD + 2)
        def _():
            pl.loop(0, SLICES)(slice_start)

        @pl.when((i >= 3) & (i < LEAD + 3))
        def _():
            stage_far(i - 3)

        @pl.when(i == 0)
        def _():
            start_acts()

        @pl.when(i == VSTART)
        def _():
            start_weights()

        @pl.when(i == 3)
        def _():
            pass_acts()

        @pl.when(i == VPASS)
        def _():
            pass_weights()

        @pl.when(i == 4)
        def _():
            finish_acts()

        @pl.when(i >= 4)
        def _():
            stage_weight_grad(i - 4)

    finish_weights()

    @pl.loop(LEAD, NZ)
    def _(k):
        wait(G.at[y, k, :, other], b_recv.at[0, k])

    @pl.loop(0, SLICES + 2)
    def _(i):
        @pl.when(i < SLICES)
        def _():
            slice_y(i)

        @pl.when((i >= 1) & (i < SLICES + 1))
        def _():
            slice_far(i - 1)

        @pl.when((i >= 2) & (i < SLICES + 2))
        def _():
            slice_input_grad(i - 2)

        @pl.when((i >= 3) & (i < SLICES + 2))
        def _():
            slice_pass(i - 3)

        @pl.when(i == SLICES + 1)
        def _():
            pl.loop(LEAD, NZ)(stage_weight_grad)

    slice_pass(SLICES - 1)
    pl.loop(0, SLICES)(slice_finish)
    wait(gw, s_recv)

    @pl.when(x != y)
    def _():
        wait(go, t_send)

    wait(V.at[pl.ds(0, 3)], v_send)
    wait(K.at[pl.ds(0, 63 * quarter)], w_send)

    wait(A.at[pl.ds(0, 3)], a_send)
    wait(G.at[0, pl.ds(0, 7), :, pl.ds(0, BLK)], z_send)
    wait(G.at[pl.ds(0, 3), pl.ds(0, 4)], y_send)
    wait(G.at[pl.ds(0, 2)], b_send)
    wait(S.at[pl.ds(0, 63)], s_send)
    wait(part.at[pl.ds(0, 3)], r_send)


def body(grad_out, acts, weight, block_mask):
    tokens, d_tile = grad_out.shape
    ff_tile = acts.shape[1]
    full_width = weight.shape[1]
    dma = pltpu.SemaphoreType.DMA
    return pl.pallas_call(
        kernel,
        out_shape=(
            jax.ShapeDtypeStruct((tokens, ff_tile), BF),
            jax.ShapeDtypeStruct((d_tile // NX, full_width), F32),
        ),
        in_specs=[pl.BlockSpec(memory_space=pltpu.HBM)] * 3 + [pl.BlockSpec(memory_space=pltpu.SMEM)],
        out_specs=(pl.BlockSpec(memory_space=pltpu.VMEM), pl.BlockSpec(memory_space=pl.ANY)),
        scratch_shapes=[
            pltpu.VMEM((NX, NZ, tokens, 2 * BLK), BF),
            pltpu.VMEM((NX, tokens, ff_tile), BF),
            pltpu.VMEM((NX, ff_tile, tokens), BF),
            pltpu.VMEM((NY, d_tile // NX, full_width // NY), BF),
            pltpu.VMEM((2 * NZ * BLK, ff_tile), BF),
            pltpu.VMEM((NX, tokens, ff_tile), F32),
            pltpu.VMEM((2, SLICES, tokens // SLICES // 2, ff_tile), F32),
            pltpu.VMEM((2, tokens, ff_tile), F32),
            pltpu.VMEM((8 * NZ, BLK // NX, ff_tile), F32),
        ] + [dma] * 9 + [dma, dma((4,)), dma, dma] + [dma((NZ,))] + [dma((LEAD,))] * 3 + [dma((SLICES,))] * 3
        + [dma((4, NZ)), dma((3, SLICES)), dma, dma((2, SLICES)), dma((SLICES,))],
        compiler_params=pltpu.CompilerParams(
            collective_id=0, has_side_effects=True, vmem_limit_bytes=63 * 1024 * 1024
        ),
    )(grad_out, acts, weight, block_mask)


def solution(mesh):
    in_specs = (P("dp", "tensor"), P("dp", "tensor"), P("tensor", None), P())
    out_specs = (P("dp", "tensor"), P(("dp", "tensor"), None))
    return jax.shard_map(body, mesh=mesh, in_specs=in_specs, out_specs=out_specs, check_vma=False)
```

time: 235 us -> 172 us (0.73)
  the two profiles are of different devices: /device:TPU:231 before, /device:TPU:8 now
where the time goes in v2:
time: 172 us; the launch traced here: 170 us
  Pallas kernels  164 us (95%)
  local copies, waits for them, and re-layouts  4.91 us (3%)
    pallas_call x1, Pallas kernels, body(): pl.pallas_call(kernel, out_shape=(jax.ShapeDtypeStruct((tokens, ff_tile),...  164 us
    unnamed x2, local copies, waits for them, and re-layouts  4.91 us

profile of v2, /device:TPU:8, one launch (start us, length us, event | category | flops | bytes accessed | tf_op | source)
XLA Modules:
  0.0 169.9 jit_solution(15656945286406690560)
XLA Ops:
  0.6 164.3 %shard_map.59 = (bf16[1024,256]{1,0:T(8,128)(2,1)}, f32[32,16384]{1,0:T(8,128)}) custom-call(bf16[1024,128]{1,0:T(8,128)(2,1)} %go.1, bf16[1024,256]{1,0:T(8,128)(2,1)} %acts.1, bf16[128,16384]{1,0:T(8,128)(2,1)} %weight.1, s32[64,128]{1,0:T(8,128)} %mask.1), custom_call_target="tpu_custom_call" | custom-call | tf_op jit(solution)/shard_map/pallas_call | solution.py:392
  165.0 1.9 %copy.8 = bf16[1024,256]{1,0:T(8,128)(2,1)} copy(bf16[1024,256]{1,0:T(8,128)(2,1)} %get-tuple-element.4) | data formatting | bytes 1048576
  166.8 3.0 %copy.9 = f32[32,16384]{1,0:T(8,128)} copy(f32[32,16384]{1,0:T(8,128)} %get-tuple-element.5) | data formatting | bytes 4194304

commit v3 on v2

--- a/solution.py
+++ b/solution.py
@@ -6,17 +6,18 @@
 from jax.sharding import PartitionSpec as P
 
 NX, NY, NZ = 4, 4, 8
-VSTART, VPASS = 1, 5
-LEAD, SLICES = 7, 4
+VSTART, VPASS = 0, 5
+LEAD, SLICES = 6, 4
 BLK = 128
 BF, F32 = jnp.bfloat16, jnp.float32
+STEPS = 32767.0
 MESH = pl.DeviceIdType.MESH
 
 
-def kernel(go, acts, weight, mask, ga, gw, G, A, At, V, K, part, H, R, S,
-           t_send, a_send, v_send, w_send, z_send, y_send, b_send, s_send, r_send,
+def kernel(go, acts, weight, mask, own, R, gw, gm, G, A, At, V, K, part, H, S, M,
+           t_send, a_send, v_send, w_send, z_send, y_send, b_send, s_send, m_send, r_send,
            t_recv, a_recv, v_recv, w_recv, z_recv, yp_recv, ym_recv, y2_recv,
-           yq_recv, yn_recv, y3_recv, b_recv, b2_recv, s_recv, h_recv, r_recv):
+           yq_recv, yn_recv, y3_recv, b_recv, b2_recv, s_recv, m_recv, h_recv, r_recv, o_recv):
     x = lax.axis_index("dp")
     t = lax.axis_index("tensor")
     y, z, c = t // (2 * NZ), (t % (2 * NZ)) // 2, t % 2
@@ -247,6 +248,10 @@
             def _():
                 send(part.at[d, rows_of(j, 0)], R.at[1, rows_of(j, 0)], r_send, r_recv.at[j], west, t)
 
+            @pl.when(rel == 2)
+            def _():
+                pltpu.make_async_copy(part.at[d, rows_of(j)], own.at[rows_of(j)], o_recv).start()
+
             @pl.when(rel == 3)
             def _():
                 send(part.at[d, rows_of(j, 1)], R.at[0, rows_of(j, 1)], r_send, r_recv.at[j], east, t)
@@ -261,8 +266,6 @@
 
     def slice_finish(j):
         wait(R.at[:, rows_of(j)], r_recv.at[j])
-        rows = rows_of(j)
-        ga[rows] = (part[x, rows] + R[0, rows] + R[1, rows]).astype(BF)
 
     scale_factor = 1.0 / (tokens * NX) ** 0.5
 
@@ -281,7 +284,12 @@
         for r in range(2):
             for h in range(2):
                 tile = total[r * BLK:(r + 1) * BLK, h * BLK:(h + 1) * BLK] * scalar(2 * zc + r, h)
-                S[pl.ds(8 * zc + 4 * r, 4), :, h * BLK:(h + 1) * BLK] = tile.reshape(4, BLK // 4, BLK)
+                tile = tile.reshape(4, BLK // 4, BLK)
+                top = jnp.max(jnp.abs(tile), axis=1, keepdims=True)
+                steps = (tile * jnp.where(top > 0, 1.0 / top, 0.0)) * STEPS
+                here = (pl.ds(8 * zc + 4 * r, 4), slice(None), slice(h * BLK, (h + 1) * BLK))
+                S[here] = jnp.round(steps).astype(jnp.int16)
+                M[here] = top
 
         @pl.loop(0, 8)
         def _(j):
@@ -290,10 +298,12 @@
             @pl.when(n == t)
             def _():
                 pltpu.make_async_copy(S.at[n], gw.at[:, columns], s_recv).start()
+                pltpu.make_async_copy(M.at[n], gm.at[:, columns], m_recv).start()
 
             @pl.when(n != t)
             def _():
                 send(S.at[n], gw.at[:, columns], s_send, s_recv, x, n)
+                send(M.at[n], gm.at[:, columns], m_send, m_recv, x, n)
 
     @pl.loop(0, LEAD + 4)
     def _(i):
@@ -368,6 +378,8 @@
     slice_pass(SLICES - 1)
     pl.loop(0, SLICES)(slice_finish)
     wait(gw, s_recv)
+    wait(gm, m_recv)
+    wait(own, o_recv)
 
     @pl.when(x != y)
     def _():
@@ -381,6 +393,7 @@
     wait(G.at[pl.ds(0, 3), pl.ds(0, 4)], y_send)
     wait(G.at[pl.ds(0, 2)], b_send)
     wait(S.at[pl.ds(0, 63)], s_send)
+    wait(M.at[pl.ds(0, 63)], m_send)
     wait(part.at[pl.ds(0, 3)], r_send)
 
 
@@ -389,14 +402,16 @@
     ff_tile = acts.shape[1]
     full_width = weight.shape[1]
     dma = pltpu.SemaphoreType.DMA
-    return pl.pallas_call(
+    own, sums, steps, top = pl.pallas_call(
         kernel,
         out_shape=(
-            jax.ShapeDtypeStruct((tokens, ff_tile), BF),
-            jax.ShapeDtypeStruct((d_tile // NX, full_width), F32),
+            jax.ShapeDtypeStruct((tokens, ff_tile), F32),
+            jax.ShapeDtypeStruct((2, tokens, ff_tile), F32),
+            jax.ShapeDtypeStruct((d_tile // NX, full_width), jnp.int16),
+            jax.ShapeDtypeStruct((1, full_width), F32),
         ),
         in_specs=[pl.BlockSpec(memory_space=pltpu.HBM)] * 3 + [pl.BlockSpec(memory_space=pltpu.SMEM)],
-        out_specs=(pl.BlockSpec(memory_space=pltpu.VMEM), pl.BlockSpec(memory_space=pl.ANY)),
+        out_specs=[pl.BlockSpec(memory_space=pltpu.HBM)] * 4,
         scratch_shapes=[
             pltpu.VMEM((NX, NZ, tokens, 2 * BLK), BF),
             pltpu.VMEM((NX, tokens, ff_tile), BF),
@@ -405,14 +420,17 @@
             pltpu.VMEM((2 * NZ * BLK, ff_tile), BF),
             pltpu.VMEM((NX, tokens, ff_tile), F32),
             pltpu.VMEM((2, SLICES, tokens // SLICES // 2, ff_tile), F32),
-            pltpu.VMEM((2, tokens, ff_tile), F32),
-            pltpu.VMEM((8 * NZ, BLK // NX, ff_tile), F32),
-        ] + [dma] * 9 + [dma, dma((4,)), dma, dma] + [dma((NZ,))] + [dma((LEAD,))] * 3 + [dma((SLICES,))] * 3
-        + [dma((4, NZ)), dma((3, SLICES)), dma, dma((2, SLICES)), dma((SLICES,))],
+            pltpu.VMEM((8 * NZ, BLK // NX, ff_tile), jnp.int16),
+            pltpu.VMEM((8 * NZ, 1, ff_tile), F32),
+        ] + [dma] * 10 + [dma, dma((4,)), dma, dma] + [dma((NZ,))] + [dma((LEAD,))] * 3 + [dma((SLICES,))] * 3
+        + [dma((4, NZ)), dma((3, SLICES)), dma, dma, dma((2, SLICES)), dma((SLICES,)), dma],
         compiler_params=pltpu.CompilerParams(
             collective_id=0, has_side_effects=True, vmem_limit_bytes=63 * 1024 * 1024
         ),
     )(grad_out, acts, weight, block_mask)
+    grad_acts = (own + sums[0] + sums[1]).astype(BF)
+    grad_weight = (steps.astype(F32) * (1.0 / STEPS)) * top
+    return grad_acts, grad_weight
 
 
 def solution(mesh):

time: 172 us -> 160 us (0.930)
  Pallas kernels: 164 us -> 153 us
  local copies, waits for them, and re-layouts: 4.91 us -> 0.01 us
  other arithmetic: 0 us -> 4.63 us
    pallas_call x1, Pallas kernels: 164 us -> 153 us  [body(): pl.pallas_call(kernel, out_shape=(jax.ShapeDtypeStruct((tokens, ff_tile),...]
    unnamed x2 -> x4, local copies, waits for them, and re-layouts: 4.91 us -> 0.01 us
    convert_element_type x0 -> x1, other arithmetic: none -> 2.9 us  [body(): grad_acts = (own + sums[0] + sums[1]).astype(BF)]
    mul x0 -> x2, other arithmetic: none -> 1.73 us  [body(): grad_weight = steps.astype(F32) * (1.0 / STEPS) * top]
where the time goes in v3:
time: 160 us; the launch traced here: 159 us
  Pallas kernels  153 us (96%)
  other arithmetic  4.63 us (3%)
    pallas_call x1, Pallas kernels, body(): pl.pallas_call(kernel, out_shape=(jax.ShapeDtypeStruct((tokens, ff_tile),...  153 us

profile of v3, /device:TPU:8, one launch (start us, length us, event | category | flops | bytes accessed | tf_op | source)
XLA Modules:
  0.0 158.6 jit_solution(1995536712662527889)
XLA Ops:
  0.6 153.3 %shard_map.59 = (f32[1024,256]{1,0:T(8,128)}, f32[2,1024,256]{2,1,0:T(8,128)}, s16[32,16384]{1,0:T(8,128)(2,1)}, f32[1,16384]{1,0:T(1,128)}) custom-call(bf16[1024,128]{1,0:T(8,128)(2,1)} %go.1, bf16[1024,256]{1,0:T(8,128)(2,1)} %acts.1, bf16[128,16384]{1,0:T(8,128)(2,1)} %weight.1, s32[64,128]{1,0:T(8,128)} %mask.1), custom_call_target="tpu_custom_call" | custom-call | tf_op jit(solution)/shard_map/pallas_call | solution.py:405
  154.0 0.0 copy-start.1
  154.0 0.0 copy-start
  154.0 2.9 %fusion = bf16[1024,256]{1,0:T(8,128)(2,1)} fusion(f32[1024,256]{1,0:T(8,128)} %get-tuple-element.6, f32[2,1024,256]{2,1,0:T(8,128)} %get-tuple-element.7), kind=kLoop, calls=%fused_computation.2 | loop fusion | flops 786432 | bytes 3670016 | tf_op jit(solution)/shard_map/convert_element_type | solution.py:431
  156.9 0.0 copy-done.1
  156.9 0.1 broadcast_multiply_fusion
  157.0 0.0 copy-done
  157.0 1.7 %convert_multiply_fusion = f32[32,16384]{1,0:T(8,128)} fusion(s16[32,16384]{1,0:T(8,128)(2,1)S(1)} %copy-done, f32[16384]{0:T(1024)S(1)} %bitcast.9), kind=kLoop, calls=%fused_computation | loop fusion | flops 1048576 | bytes 3211264 | tf_op jit(solution)/shard_map/mul | solution.py:432
Async XLA Ops:
  154.0 2.9 %copy-start.1 = (f32[1,16384]{1,0:T(1,128)S(1)}, f32[1,16384]{1,0:T(1,128)}, u32[]{:S(2)}) copy-start(f32[1,16384]{1,0:T(1,128)} %get-tuple-element.9) | copy-start | bytes 196612
  154.0 3.0 %copy-start = (s16[32,16384]{1,0:T(8,128)(2,1)S(1)}, s16[32,16384]{1,0:T(8,128)(2,1)}, u32[]{:S(2)}) copy-start(s16[32,16384]{1,0:T(8,128)(2,1)} %get-tuple-element.8) | copy-start | bytes 3145732

commit v4 on v3

--- a/solution.py
+++ b/solution.py
@@ -74,15 +74,15 @@
     def _():
         pl.semaphore_wait(barrier, greeted)
 
-    home = G.at[x, 0, :, mine]
-
-    @pl.when(x != y)
-    def _():
-        send(go, home, t_send, t_recv, y, x * 2 * NZ + z * 2 + c)
-
-    @pl.when(x == y)
-    def _():
-        pltpu.make_async_copy(go, home, t_recv).start()
+
+    for part_of, rows in enumerate((low, high)):
+        @pl.when(x != y)
+        def _():
+            send(go.at[rows], G.at[x, 0, rows, mine], t_send, t_recv.at[part_of], y, partner)
+
+        @pl.when(x == y)
+        def _():
+            pltpu.make_async_copy(go.at[rows], G.at[x, 0, rows, mine], t_recv.at[part_of]).start()
 
     east, west = (x + 1) % NX, (x + NX - 1) % NX
     pltpu.make_async_copy(acts, A.at[x], a_recv.at[0]).start()
@@ -154,7 +154,11 @@
 
         @pl.when(k == 0)
         def _():
-            wait(block, t_recv)
+            for part_of, rows in enumerate((low, high)):
+                piece = G.at[y, k, rows, mine]
+                wait(piece, t_recv.at[part_of])
+                send(piece, piece, y_send, yp_recv.at[k], x, up)
+                send(piece, piece, y_send, ym_recv.at[k], x, down)
 
         @pl.when(k > 0)
         def _():
@@ -169,7 +173,7 @@
         def _():
             send(block, G.at[y, k + 2, :, mine], z_send, z_recv.at[k + 2], x, left)
 
-        @pl.when(k < LEAD)
+        @pl.when((k > 0) & (k < LEAD))
         def _():
             send(block, block, y_send, yp_recv.at[k], x, up)
             send(block, block, y_send, ym_recv.at[k], x, down)
@@ -347,12 +351,6 @@
         def _():
             stage_weight_grad(i - 4)
 
-    finish_weights()
-
-    @pl.loop(LEAD, NZ)
-    def _(k):
-        wait(G.at[y, k, :, other], b_recv.at[0, k])
-
     @pl.loop(0, SLICES + 2)
     def _(i):
         @pl.when(i < SLICES)
@@ -362,6 +360,14 @@
         @pl.when((i >= 1) & (i < SLICES + 1))
         def _():
             slice_far(i - 1)
+
+        @pl.when(i == 2)
+        def _():
+            finish_weights()
+
+            @pl.loop(LEAD, NZ)
+            def _(k):
+                wait(G.at[y, k, :, other], b_recv.at[0, k])
 
         @pl.when((i >= 2) & (i < SLICES + 2))
         def _():
@@ -422,7 +428,7 @@
             pltpu.VMEM((2, SLICES, tokens // SLICES // 2, ff_tile), F32),
             pltpu.VMEM((8 * NZ, BLK // NX, ff_tile), jnp.int16),
             pltpu.VMEM((8 * NZ, 1, ff_tile), F32),
-        ] + [dma] * 10 + [dma, dma((4,)), dma, dma] + [dma((NZ,))] + [dma((LEAD,))] * 3 + [dma((SLICES,))] * 3
+        ] + [dma] * 10 + [dma((2,)), dma((4,)), dma, dma] + [dma((NZ,))] + [dma((LEAD,))] * 3 + [dma((SLICES,))] * 3
         + [dma((4, NZ)), dma((3, SLICES)), dma, dma, dma((2, SLICES)), dma((SLICES,)), dma],
         compiler_params=pltpu.CompilerParams(
             collective_id=0, has_side_effects=True, vmem_limit_bytes=63 * 1024 * 1024

time: 160 us -> 156 us (0.975)
  Pallas kernels: 153 us -> 151 us
    pallas_call x1, Pallas kernels: 153 us -> 151 us  [body(): pl.pallas_call(kernel, out_shape=(jax.ShapeDtypeStruct((tokens, ff_tile),...]
where the time goes in v4:
time: 156 us
  Pallas kernels  151 us (97%)
  other arithmetic  4.63 us (3%)
    pallas_call x1, Pallas kernels, body(): pl.pallas_call(kernel, out_shape=(jax.ShapeDtypeStruct((tokens, ff_tile),...  151 us

profile of v4, /device:TPU:8, one launch (start us, length us, event | category | flops | bytes accessed | tf_op | source)
XLA Modules:
  0.0 155.8 jit_solution(1400545125815329154)
XLA Ops:
  0.6 150.5 %shard_map.59 = (f32[1024,256]{1,0:T(8,128)}, f32[2,1024,256]{2,1,0:T(8,128)}, s16[32,16384]{1,0:T(8,128)(2,1)}, f32[1,16384]{1,0:T(1,128)}) custom-call(bf16[1024,128]{1,0:T(8,128)(2,1)} %go.1, bf16[1024,256]{1,0:T(8,128)(2,1)} %acts.1, bf16[128,16384]{1,0:T(8,128)(2,1)} %weight.1, s32[64,128]{1,0:T(8,128)} %mask.1), custom_call_target="tpu_custom_call" | custom-call | tf_op jit(solution)/shard_map/pallas_call | solution.py:411
  151.2 0.0 copy-start.1
  151.2 0.0 copy-start
  151.2 2.9 %fusion = bf16[1024,256]{1,0:T(8,128)(2,1)} fusion(f32[1024,256]{1,0:T(8,128)} %get-tuple-element.6, f32[2,1024,256]{2,1,0:T(8,128)} %get-tuple-element.7), kind=kLoop, calls=%fused_computation.2 | loop fusion | flops 786432 | bytes 3670016 | tf_op jit(solution)/shard_map/convert_element_type | solution.py:437
  154.1 0.0 copy-done.1
  154.1 0.1 broadcast_multiply_fusion
  154.2 0.0 copy-done
  154.2 1.7 %convert_multiply_fusion = f32[32,16384]{1,0:T(8,128)} fusion(s16[32,16384]{1,0:T(8,128)(2,1)S(1)} %copy-done, f32[16384]{0:T(1024)S(1)} %bitcast.9), kind=kLoop, calls=%fused_computation | loop fusion | flops 1048576 | bytes 3211264 | tf_op jit(solution)/shard_map/mul | solution.py:438
Async XLA Ops:
  151.2 2.9 %copy-start.1 = (f32[1,16384]{1,0:T(1,128)S(1)}, f32[1,16384]{1,0:T(1,128)}, u32[]{:S(2)}) copy-start(f32[1,16384]{1,0:T(1,128)} %get-tuple-element.9) | copy-start | bytes 196612
  151.2 3.0 %copy-start = (s16[32,16384]{1,0:T(8,128)(2,1)S(1)}, s16[32,16384]{1,0:T(8,128)(2,1)}, u32[]{:S(2)}) copy-start(s16[32,16384]{1,0:T(8,128)(2,1)} %get-tuple-element.8) | copy-start | bytes 3145732

commit v5 on v4

--- a/solution.py
+++ b/solution.py
@@ -6,8 +6,8 @@
 from jax.sharding import PartitionSpec as P
 
 NX, NY, NZ = 4, 4, 8
-VSTART, VPASS = 0, 5
-LEAD, SLICES = 6, 4
+VPASS = 5
+LEAD, SLICES = 5, 4
 BLK = 128
 BF, F32 = jnp.bfloat16, jnp.float32
 STEPS = 32767.0
@@ -146,6 +146,8 @@
                 cols = slice(h * BLK, (h + 1) * BLK)
                 K[rows, cols] = (K[rows, cols].astype(F32) * scalar(f, h)).astype(BF)
 
+    start_weights()
+
     def chunk(k):
         return (z + NZ + ((k + 1) // 2) * (1 - 2 * (k % 2))) % NZ
 
@@ -330,10 +332,6 @@
         @pl.when(i == 0)
         def _():
             start_acts()
-
-        @pl.when(i == VSTART)
-        def _():
-            start_weights()
 
         @pl.when(i == 3)
         def _():

time: 156 us -> 153 us (0.981)
  Pallas kernels: 151 us -> 148 us
    pallas_call x1, Pallas kernels: 151 us -> 148 us  [body(): pl.pallas_call(kernel, out_shape=(jax.ShapeDtypeStruct((tokens, ff_tile),...]
where the time goes in v5:
time: 153 us
  Pallas kernels  148 us (97%)
  other arithmetic  4.63 us (3%)
    pallas_call x1, Pallas kernels, body(): pl.pallas_call(kernel, out_shape=(jax.ShapeDtypeStruct((tokens, ff_tile),...  148 us

profile of v5, /device:TPU:8, one launch (start us, length us, event | category | flops | bytes accessed | tf_op | source)
XLA Modules:
  0.0 153.0 jit_solution(14322301237271929827)
XLA Ops:
  0.6 147.7 %shard_map.59 = (f32[1024,256]{1,0:T(8,128)}, f32[2,1024,256]{2,1,0:T(8,128)}, s16[32,16384]{1,0:T(8,128)(2,1)}, f32[1,16384]{1,0:T(1,128)}) custom-call(bf16[1024,128]{1,0:T(8,128)(2,1)} %go.1, bf16[1024,256]{1,0:T(8,128)(2,1)} %acts.1, bf16[128,16384]{1,0:T(8,128)(2,1)} %weight.1, s32[64,128]{1,0:T(8,128)} %mask.1), custom_call_target="tpu_custom_call" | custom-call | tf_op jit(solution)/shard_map/pallas_call | solution.py:409
  148.3 0.0 copy-start.1
  148.3 0.0 copy-start
  148.3 2.9 %fusion = bf16[1024,256]{1,0:T(8,128)(2,1)} fusion(f32[1024,256]{1,0:T(8,128)} %get-tuple-element.6, f32[2,1024,256]{2,1,0:T(8,128)} %get-tuple-element.7), kind=kLoop, calls=%fused_computation.2 | loop fusion | flops 786432 | bytes 3670016 | tf_op jit(solution)/shard_map/convert_element_type | solution.py:435
  151.2 0.0 copy-done.1
  151.2 0.1 broadcast_multiply_fusion
  151.3 0.0 copy-done
  151.3 1.7 %convert_multiply_fusion = f32[32,16384]{1,0:T(8,128)} fusion(s16[32,16384]{1,0:T(8,128)(2,1)S(1)} %copy-done, f32[16384]{0:T(1024)S(1)} %bitcast.9), kind=kLoop, calls=%fused_computation | loop fusion | flops 1048576 | bytes 3211264 | tf_op jit(solution)/shard_map/mul | solution.py:436
Async XLA Ops:
  148.3 2.9 %copy-start.1 = (f32[1,16384]{1,0:T(1,128)S(1)}, f32[1,16384]{1,0:T(1,128)}, u32[]{:S(2)}) copy-start(f32[1,16384]{1,0:T(1,128)} %get-tuple-element.9) | copy-start | bytes 196612
  148.3 3.0 %copy-start = (s16[32,16384]{1,0:T(8,128)(2,1)S(1)}, s16[32,16384]{1,0:T(8,128)(2,1)}, u32[]{:S(2)}) copy-start(s16[32,16384]{1,0:T(8,128)(2,1)} %get-tuple-element.8) | copy-start | bytes 3145732

commit v6 on v5

--- a/solution.py
+++ b/solution.py
@@ -333,7 +333,7 @@
         def _():
             start_acts()
 
-        @pl.when(i == 3)
+        @pl.when(i == 2)
         def _():
             pass_acts()
 

time: 153 us -> 153 us (level)
  no operation moved by 1% of the time
where the time goes in v6:
time: 153 us
  Pallas kernels  147 us (96%)
  other arithmetic  4.63 us (3%)
    pallas_call x1, Pallas kernels, body(): pl.pallas_call(kernel, out_shape=(jax.ShapeDtypeStruct((tokens, ff_tile),...  147 us

profile of v6, /device:TPU:8, one launch (start us, length us, event | category | flops | bytes accessed | tf_op | source)
XLA Modules:
  0.0 152.6 jit_solution(11885756381711665621)
XLA Ops:
  0.6 147.3 %shard_map.59 = (f32[1024,256]{1,0:T(8,128)}, f32[2,1024,256]{2,1,0:T(8,128)}, s16[32,16384]{1,0:T(8,128)(2,1)}, f32[1,16384]{1,0:T(1,128)}) custom-call(bf16[1024,128]{1,0:T(8,128)(2,1)} %go.1, bf16[1024,256]{1,0:T(8,128)(2,1)} %acts.1, bf16[128,16384]{1,0:T(8,128)(2,1)} %weight.1, s32[64,128]{1,0:T(8,128)} %mask.1), custom_call_target="tpu_custom_call" | custom-call | tf_op jit(solution)/shard_map/pallas_call | solution.py:409
  147.9 0.0 copy-start.1
  148.0 0.0 copy-start
  148.0 2.9 %fusion = bf16[1024,256]{1,0:T(8,128)(2,1)} fusion(f32[1024,256]{1,0:T(8,128)} %get-tuple-element.6, f32[2,1024,256]{2,1,0:T(8,128)} %get-tuple-element.7), kind=kLoop, calls=%fused_computation.2 | loop fusion | flops 786432 | bytes 3670016 | tf_op jit(solution)/shard_map/convert_element_type | solution.py:435
  150.9 0.0 copy-done.1
  150.9 0.1 broadcast_multiply_fusion
  150.9 0.0 copy-done
  151.0 1.7 %convert_multiply_fusion = f32[32,16384]{1,0:T(8,128)} fusion(s16[32,16384]{1,0:T(8,128)(2,1)S(1)} %copy-done, f32[16384]{0:T(1024)S(1)} %bitcast.9), kind=kLoop, calls=%fused_computation | loop fusion | flops 1048576 | bytes 3211264 | tf_op jit(solution)/shard_map/mul | solution.py:436
Async XLA Ops:
  147.9 2.9 %copy-start.1 = (f32[1,16384]{1,0:T(1,128)S(1)}, f32[1,16384]{1,0:T(1,128)}, u32[]{:S(2)}) copy-start(f32[1,16384]{1,0:T(1,128)} %get-tuple-element.9) | copy-start | bytes 196612
  148.0 3.0 %copy-start = (s16[32,16384]{1,0:T(8,128)(2,1)S(1)}, s16[32,16384]{1,0:T(8,128)(2,1)}, u32[]{:S(2)}) copy-start(s16[32,16384]{1,0:T(8,128)(2,1)} %get-tuple-element.8) | copy-start | bytes 3145732
